TPU v7x, 32 devices: a whole 2x2x4 slice. The times are simulated.
32 devices in a mesh: groups: 2 (over x), ctx: 16 (over z, y, core).
Axes of the slice: x: 2, y: 2, z: 4, core: 2. Of those that a mesh axis runs over, the one named last changes fastest.
Arguments:
- tokens: bfloat16 [16384, 1024], P(('groups', 'ctx')), parts along dimension 0
- w_qkv: bfloat16 [1024, 3072], P('ctx'), may hold values from -0.1875 to 0.1875
- w_out: bfloat16 [1024, 1024], P('ctx'), may hold values from -0.1875 to 0.1875
- var_bias: float32 [2, 16], replicated, may hold values from -2 to 2
- seg_id: int32 [16384], P(('groups', 'ctx')), parts along dimension 0, may hold values from 0 to 3, as said below
- var_id: int32 [16384], P(('groups', 'ctx')), parts along dimension 0, may hold values from 0 to 511
- time_id: int32 [16384], P(('groups', 'ctx')), parts along dimension 0, may hold values from 0 to 67
Outputs:
- mixed: bfloat16 [16384, 1024], P(('groups', 'ctx')), parts along dimension 0
There are 2 independent parts, one for each index of `groups`. A program takes and returns all parts, laid end to end along the dimension named above; an argument that names none is the same for every part. Nothing has to cross between parts.
Inputs may be any that keep to these rules, and one draw needn't show every extreme that they name: seg_id starts at 0, never falls, and rises by at most one from a token to the next.
All inputs are finite; a program needn't handle non-finite values.
Results may differ from a plain program's by a relative error of at most 0.004.
The roundings to bfloat16 on the way count: a program that leaves them out, or rounds other values in their place, can miss the bound.
Values may be sent and summed in bfloat16 or wider, within the bound.
No kernel may reach another device: no remote copies, remote signals or barrier semaphores. Data moves between devices by JAX's collectives and lax.ppermute only.
A program may use at most 256 MiB of HBM per device.

v0:
```python
import math
import jax
import jax.numpy as jnp
from jax import lax
from jax.sharding import PartitionSpec as P


def as_sent(value):
    return jax.tree.map(lambda a: a.astype(jnp.bfloat16) if a.dtype == jnp.float32 else a, value)


def passed_along(value, axis, by):
    devices = lax.axis_size(axis)
    return lax.ppermute(value, axis, [(i, (i + by) % devices) for i in range(devices)])


def gather_near(payload):

    def relay(item, step):
        return passed_along((item[0], as_sent(item[1])), "ctx", step)

    before_one = relay(payload, 1)
    before_two = relay(before_one, 1)
    after_one = relay(payload, -1)
    after_two = relay(after_one, -1)
    return (before_two, before_one, after_one, after_two)


def local(tokens, w_qkv, w_out, var_bias, seg_id, var_id, time_id):
    rows = tokens.shape[0]
    width = tokens.shape[1]
    heads = var_bias.shape[1]
    hsize = width // heads
    idents = jnp.stack([seg_id, var_id, time_id], 0)
    center = lax.axis_index("ctx")
    count = lax.axis_size("ctx")
    columns = tokens
    qkv = jnp.dot(
        columns,
        lax.all_gather(w_qkv, "ctx", axis=0, tiled=True),
        preferred_element_type=jnp.float32,
    )
    qkv = qkv.astype(jnp.bfloat16)
    query = qkv[:, :width]
    keyval = qkv[:, width:]
    near = gather_near((keyval, idents))
    kv_list = [near[0][0], near[1][0], keyval, near[2][0], near[3][0]]
    id_list = [near[0][1], near[1][1], idents, near[2][1], near[3][1]]
    win_kv = jnp.concatenate(kv_list, 0)
    win_ids = jnp.concatenate(id_list, 1)
    span = 5 * rows
    q_pos = center * rows + jnp.arange(rows, dtype=jnp.int32)
    k_pos = (center - 2) * rows + jnp.arange(span, dtype=jnp.int32)
    inside = (k_pos >= 0) & (k_pos < count * rows)
    allowed = (seg_id[:, None] == win_ids[0][None, :]) & (win_ids[2][None, :] <= time_id[:, None])
    allowed = allowed & (jnp.abs(q_pos[:, None] - k_pos[None, :]) <= 2 * rows - 1) & inside[None, :]
    same = var_id[:, None] == win_ids[1][None, :]
    query_heads = query.reshape(rows, heads, hsize)
    key_heads = win_kv[:, :width].reshape(span, heads, hsize)
    value_heads = win_kv[:, width:].reshape(span, heads, hsize)
    scale = 1.0 / math.sqrt(hsize)
    group = math.gcd(4, heads)
    results = []
    for first in range(0, heads, group):
        q_grp = query_heads[:, first : first + group]
        k_grp = key_heads[:, first : first + group]
        v_grp = value_heads[:, first : first + group]
        bias = jnp.where(
            same[None, :, :],
            var_bias[0, first : first + group][:, None, None],
            var_bias[1, first : first + group][:, None, None],
        )
        score = (
            jnp.einsum("qhe,khe->hqk", q_grp, k_grp, preferred_element_type=jnp.float32) * scale
            + bias
        )
        score = jnp.where(allowed[None, :, :], score, -1e30)
        peak = jnp.max(score, axis=-1, keepdims=True)
        weight = jnp.where(allowed[None, :, :], jnp.exp(score - peak), 0.0)
        total = jnp.sum(weight, axis=-1)
        weight_bf = weight.astype(jnp.bfloat16)
        summed = jnp.einsum("hqk,khe->qhe", weight_bf, v_grp, preferred_element_type=jnp.float32)
        results.append(summed / jnp.transpose(total)[:, :, None])
    attended = jnp.concatenate(results, 1).reshape(rows, width).astype(jnp.bfloat16)
    columns = attended
    mixed = jnp.dot(
        columns,
        lax.all_gather(w_out, "ctx", axis=0, tiled=True),
        preferred_element_type=jnp.float32,
    )
    return mixed.astype(jnp.bfloat16)


def solution(mesh):
    in_specs = (
        P(("groups", "ctx"), None),
        P("ctx", None),
        P("ctx", None),
        P(),
        P(("groups", "ctx")),
        P(("groups", "ctx")),
        P(("groups", "ctx")),
    )
    out_specs = P(("groups", "ctx"), None)
    return jax.shard_map(local, mesh=mesh, in_specs=in_specs, out_specs=out_specs, check_vma=False)
```

profile of v0, /device:TPU:1, one launch (start us, length us, event | category | flops | bytes accessed | tf_op | source)
XLA Modules:
  0.0 518.6 jit_solution(13979249160202723776)
XLA Ops:
  6.5 0.0 copy-start
  6.5 0.0 all-gather.3.cloned.1.call-start
  6.5 0.7 all-gather.3.cloned.1.call-update
  7.3 0.0 copy-start.6
  7.3 0.0 copy-start.7
  7.3 0.0 copy-start.8
  7.3 0.0 copy-start.9
  7.3 0.0 all-gather.5.cloned.1.call-start
  7.3 66.7 %all-gather.3.cloned.1.call-done = bf16[1024,3072]{1,0:T(8,128)(2,1)} async-done(((bf16[64,3072]{1,0:T(8,128)(2,1)}), bf16[1024,3072]{1,0:T(8,128)(2,1)}) %all-gather.3.cloned.1.call-update) | async-done | bytes 6291472 | tf_op jit(solution)/shard_map/all_gather | solution.py:40
  74.0 0.0 copy-done
  74.0 6.4 %convolution_convert_fusion = bf16[512,3072]{1,0:T(8,128)(2,1)S(1)} fusion(bf16[512,1024]{1,0:T(8,128)(2,1)S(1)} %copy-done, bf16[1024,3072]{1,0:T(8,128)(2,1)} %all-gather.3.cloned.1.call-done), kind=kOutput, calls=%fused_computation.51 | convolution fusion | flops 3222798336 | bytes 10485760 | tf_op jit(solution)/shard_map/dot_general | solution.py:38
  80.4 0.0 copy-start.2
  80.4 1.7 copy-done.2
  82.2 1.5 slice.117
  83.7 0.4 collective-permute-start
  84.1 0.1 collective-permute-start.2
  84.2 0.0 copy-done.6
  84.2 1.7 collective-permute-start.4
  85.9 2.6 collective-permute-start.6
  88.5 0.0 all-gather.5.cloned.1.call-update
  88.6 0.0 copy-done.9
  88.6 0.6 slice_bitcast_fusion.7
  89.2 47.8 %collective-permute-done.4 = s32[3,512]{1,0:T(4,128)S(1)} collective-permute-done((s32[3,512]{1,0:T(4,128)S(1)}, s32[3,512]{1,0:T(4,128)S(1)}, u32[]{:S(2)}, u32[]{:S(2)}) %collective-permute-start.4) | collective-permute-done | bytes 6176 | tf_op jit(solution)/shard_map/ppermute | solution.py:14
  137.0 2.5 collective-permute-start.5
  139.4 0.5 collective-permute-done.6
  139.9 0.0 collective-permute-start.7
  139.9 0.0 collective-permute-done
  139.9 1.7 collective-permute-start.1
  141.7 0.0 collective-permute-done.5
  141.7 2.5 collective-permute-done.7
  144.2 0.1 slice_reduce_fusion.2
  144.3 5.6 %fusion.41 = pred[512,2560]{1,0:T(8,128)(4,1)} fusion(s32[2560]{0:T(1024)S(1)} %iota_add_fusion, s32[512]{0:T(512)S(1)} %iota_add_fusion.1, s32[2560]{0:T(1024)S(1)} %get-tuple-element.7, s32[2560]{0:T(1024)S(1)} %get-tuple-element.5, s32[512]{0:T(512)S(1)} %copy-done.6, s32[512]{0:T(512)S(1)} %copy-done.7, pred[2560]{0:T(1024)(128)(4,1)S(1)} %compare_and_fusion), kind=kLoop, calls=%fused_computation.50 | loop fusion | flops 10485760 | bytes 1350144 | tf_op jit(solution)/shard_map/and | solution.py:56
  149.9 0.0 collective-permute-done.2
  149.9 0.5 collective-permute-start.3
  150.3 2.0 broadcast_compare_fusion
  152.3 1.3 slice.121
  153.6 1.3 copy.21
  154.9 32.5 %collective-permute-done.1 = bf16[512,2048]{1,0:T(8,128)(2,1)} collective-permute-done((bf16[512,2048]{1,0:T(8,128)(2,1)}, bf16[512,2048]{1,0:T(8,128)(2,1)}, u32[]{:S(2)}, u32[]{:S(2)}) %collective-permute-start.1) | collective-permute-done | bytes 2097184 | tf_op jit(solution)/shard_map/ppermute | solution.py:14
  187.4 3.2 constant_dynamic-update-slice_fusion.4
  190.6 3.1 constant_dynamic-update-slice_fusion.3
  193.7 3.2 constant_dynamic-update-slice_fusion.2
  196.9 1.5 constant_dynamic-update-slice_fusion.1
  198.4 0.0 collective-permute-done.3
  198.4 3.2 constant_dynamic-update-slice_fusion
  201.6 9.2 %fusion.118 = (bf16[2560,1024]{1,0:T(8,128)(2,1)}, bf16[2560,1024]{1,0:T(8,128)(2,1)}) fusion(bf16[2560,2048]{1,0:T(8,128)(2,1)} %constant_dynamic-update-slice_fusion), kind=kLoop, calls=%fused_computation.124 | loop fusion | bytes 20971520 | tf_op jit(solution)/shard_map/slice | solution.py:59
  210.9 8.0 %copy.22 = bf16[2560,1024]{0,1:T(8,128)(2,1)} copy(bf16[2560,1024]{1,0:T(8,128)(2,1)} %get-tuple-element.8) | data formatting | bytes 10485760 | tf_op jit(solution)/shard_map/slice | solution.py:59
  218.9 0.0 copy-done.5
  218.9 10.1 %fusion.42 = f32[4,512,2560]{2,1,0:T(8,128)} fusion(bf16[512,16,64]{0,2,1:T(8,128)(2,1)S(1)} %bitcast.72, bf16[2560,16,64]{0,2,1:T(8,128)(2,1)} %bitcast.67), kind=kOutput, calls=%fused_computation.54 | convolution fusion | flops 671088640 | bytes 23330816 | tf_op jit(solution)/shard_map/qhe,khe->hqk/dot_general | solution.py:74
  229.0 8.8 %fusion.44 = f32[4,512,2560]{2,1,0:T(8,128)} fusion(bf16[512,16,64]{0,2,1:T(8,128)(2,1)S(1)} %bitcast.73, bf16[2560,16,64]{0,2,1:T(8,128)(2,1)S(1)} %bitcast.68), kind=kOutput, calls=%fused_computation.56 | convolution fusion | flops 671088640 | bytes 23330816 | tf_op jit(solution)/shard_map/qhe,khe->hqk/dot_general | solution.py:74
  237.8 8.6 %fusion.46 = f32[4,512,2560]{2,1,0:T(8,128)} fusion(bf16[512,16,64]{0,2,1:T(8,128)(2,1)S(1)} %bitcast.74, bf16[2560,16,64]{0,2,1:T(8,128)(2,1)S(1)} %bitcast.69), kind=kOutput, calls=%fused_computation.58 | convolution fusion | flops 671088640 | bytes 23330816 | tf_op jit(solution)/shard_map/qhe,khe->hqk/dot_general | solution.py:74
  246.4 8.7 %fusion.48 = f32[4,512,2560]{2,1,0:T(8,128)} fusion(bf16[512,16,64]{0,2,1:T(8,128)(2,1)S(1)} %bitcast.75, bf16[2560,16,64]{0,2,1:T(8,128)(2,1)S(1)} %bitcast.70), kind=kOutput, calls=%fused_computation.60 | convolution fusion | flops 671088640 | bytes 23330816 | tf_op jit(solution)/shard_map/qhe,khe->hqk/dot_general | solution.py:74
  255.1 7.9 %copy.20 = bf16[2560,1024]{0,1:T(8,128)(2,1)} copy(bf16[2560,1024]{1,0:T(8,128)(2,1)} %get-tuple-element.9) | data formatting | bytes 10485760 | tf_op jit(solution)/shard_map/slice | solution.py:60
  263.0 31.4 %fusion.119 = f32[4,512]{1,0:T(4,128)S(1)} fusion(f32[4,512,2560]{2,1,0:T(8,128)} %fusion.42, f32[4]{0:T(128)S(1)} %get-tuple-element.16, f32[4]{0:T(128)S(1)} %get-tuple-element.17, pred[512,2560]{1,0:T(8,128)(4,1)} %broadcast_compare_fusion, pred[512,2560]{1,0:T(8,128)(4,1)S(1)} %copy-done.4), kind=kOutput, calls=%fused_computation.125 | output fusion | flops 36702720 | bytes 23601184 | tf_op jit(solution)/shard_map/sub | solution.py:79
  294.4 29.6 %fusion.65 = bf16[512,4,64]{0,2,1:T(8,128)(2,1)S(1)} fusion(bf16[2560,16,64]{0,2,1:T(8,128)(2,1)} %bitcast.63, f32[4,512,2560]{2,1,0:T(8,128)} %fusion.42, f32[4]{0:T(128)S(1)} %get-tuple-element.16, f32[4]{0:T(128)S(1)} %get-tuple-element.17, pred[512,2560]{1,0:T(8,128)(4,1)} %broadcast_compare_fusion, pred[512,2560]{1,0:T(8,128)(4,1)S(1)} %copy-done.4, ...), kind=kOutput, calls=%fused_computation.68 | convolution fusion | flops 708055552 | bytes 29106208 | tf_op jit(solution)/shard_map/hqk,khe->qhe/dot_general | solution.py:82
  324.0 31.1 %fusion.120 = f32[4,512]{1,0:T(4,128)S(1)} fusion(f32[4,512,2560]{2,1,0:T(8,128)} %fusion.44, f32[4]{0:T(128)S(1)} %get-tuple-element.11, f32[4]{0:T(128)S(1)} %get-tuple-element.12, pred[512,2560]{1,0:T(8,128)(4,1)} %broadcast_compare_fusion, pred[512,2560]{1,0:T(8,128)(4,1)S(1)} %copy-done.4), kind=kOutput, calls=%fused_computation.126 | output fusion | flops 36702720 | bytes 23601184 | tf_op jit(solution)/shard_map/sub | solution.py:79
  355.1 29.7 %fusion.71 = bf16[512,4,64]{0,2,1:T(8,128)(2,1)S(1)} fusion(bf16[2560,16,64]{0,2,1:T(8,128)(2,1)} %bitcast.64, f32[4,512,2560]{2,1,0:T(8,128)} %fusion.44, f32[4]{0:T(128)S(1)} %get-tuple-element.11, f32[4]{0:T(128)S(1)} %get-tuple-element.12, pred[512,2560]{1,0:T(8,128)(4,1)} %broadcast_compare_fusion, pred[512,2560]{1,0:T(8,128)(4,1)S(1)} %copy-done.4, ...), kind=kOutput, calls=%fused_computation.70 | convolution fusion | flops 708055552 | bytes 29106208 | tf_op jit(solution)/shard_map/hqk,khe->qhe/dot_general | solution.py:82
  384.8 31.7 %fusion.121 = f32[4,512]{1,0:T(4,128)S(1)} fusion(f32[4,512,2560]{2,1,0:T(8,128)} %fusion.46, f32[4]{0:T(128)S(1)} %get-tuple-element.13, f32[4]{0:T(128)S(1)} %get-tuple-element.14, pred[512,2560]{1,0:T(8,128)(4,1)} %broadcast_compare_fusion, pred[512,2560]{1,0:T(8,128)(4,1)S(1)} %copy-done.4), kind=kOutput, calls=%fused_computation.127 | output fusion | flops 36702720 | bytes 23601184 | tf_op jit(solution)/shard_map/sub | solution.py:79
  416.5 29.5 %fusion.77 = bf16[512,4,64]{0,2,1:T(8,128)(2,1)S(1)} fusion(bf16[2560,16,64]{0,2,1:T(8,128)(2,1)} %bitcast.65, f32[4,512,2560]{2,1,0:T(8,128)} %fusion.46, f32[4]{0:T(128)S(1)} %get-tuple-element.13, f32[4]{0:T(128)S(1)} %get-tuple-element.14, pred[512,2560]{1,0:T(8,128)(4,1)} %broadcast_compare_fusion, pred[512,2560]{1,0:T(8,128)(4,1)S(1)} %copy-done.4, ...), kind=kOutput, calls=%fused_computation.72 | convolution fusion | flops 708055552 | bytes 29106208 | tf_op jit(solution)/shard_map/hqk,khe->qhe/dot_general | solution.py:82
  446.0 31.6 %fusion.122 = f32[4,512]{1,0:T(4,128)S(1)} fusion(f32[4,512,2560]{2,1,0:T(8,128)} %fusion.48, f32[4]{0:T(128)S(1)} %copy-done.11, f32[4]{0:T(128)S(1)} %copy-done.10, pred[512,2560]{1,0:T(8,128)(4,1)} %broadcast_compare_fusion, pred[512,2560]{1,0:T(8,128)(4,1)S(1)} %copy-done.4), kind=kOutput, calls=%fused_computation.128 | output fusion | flops 36702720 | bytes 23601184 | tf_op jit(solution)/shard_map/sub | solution.py:79
  477.6 0.0 copy-start.1
  477.6 29.9 %fusion.83 = bf16[512,4,64]{0,2,1:T(8,128)(2,1)S(1)} fusion(bf16[2560,16,64]{0,2,1:T(8,128)(2,1)} %bitcast.66, f32[4,512,2560]{2,1,0:T(8,128)} %fusion.48, f32[4]{0:T(128)S(1)} %copy-done.11, f32[4]{0:T(128)S(1)} %copy-done.10, pred[512,2560]{1,0:T(8,128)(4,1)} %broadcast_compare_fusion, pred[512,2560]{1,0:T(8,128)(4,1)S(1)} %copy-done.4, ...), kind=kOutput, calls=%fused_computation.74 | convolution fusion | flops 708055552 | bytes 29106208 | tf_op jit(solution)/shard_map/hqk,khe->qhe/dot_general | solution.py:82
  507.5 0.1 pad_maximum_fusion
  507.7 0.0 all-gather.5.cloned.1.call-done
  507.7 3.8 convolution_convert_fusion.1
  (21 shorter events, 0.1 us)
Async XLA Ops:
  6.5 67.5 %copy-start = (bf16[512,1024]{1,0:T(8,128)(2,1)S(1)}, bf16[512,1024]{1,0:T(8,128)(2,1)}, u32[]{:S(2)}) copy-start(bf16[512,1024]{1,0:T(8,128)(2,1)} %param.7) | copy-start | bytes 3145732
  6.5 67.5 %all-gather.3.cloned.1.call-start = ((), (), s32[]{:S(2)}) async-start(), calls=%async_computation | async-start | bytes 6684672 | tf_op jit(solution)/shard_map/all_gather | solution.py:40
  7.3 76.9 %copy-start.6 = (s32[512]{0:T(512)S(1)}, s32[512]{0:T(512)}, u32[]{:S(2)}) copy-start(s32[512]{0:T(512)} %param.13) | copy-start | bytes 6148
  7.3 76.9 %copy-start.7 = (s32[512]{0:T(512)S(1)}, s32[512]{0:T(512)}, u32[]{:S(2)}) copy-start(s32[512]{0:T(512)} %param.11) | copy-start | bytes 6148
  7.3 76.9 %copy-start.8 = (s32[512]{0:T(512)S(1)}, s32[512]{0:T(512)}, u32[]{:S(2)}) copy-start(s32[512]{0:T(512)} %param.12) | copy-start | bytes 6148
  7.3 81.3 %copy-start.9 = (f32[2,16]{1,0:T(2,128)S(1)}, f32[2,16]{1,0:T(2,128)}, u32[]{:S(2)}) copy-start(f32[2,16]{1,0:T(2,128)} %param.10) | copy-start | bytes 388
  7.3 500.4 %all-gather.5.cloned.1.call-start = ((), (), s32[]{:S(2)}) async-start(), calls=%async_computation.1 | async-start | bytes 2228224 | tf_op jit(solution)/shard_map/all_gather | solution.py:88
  80.4 1.8 copy-start.2
  83.7 56.2 %collective-permute-start = (bf16[512,2048]{1,0:T(8,128)(2,1)}, bf16[512,2048]{1,0:T(8,128)(2,1)}, u32[]{:S(2)}, u32[]{:S(2)}) collective-permute-start(bf16[512,2048]{1,0:T(8,128)(2,1)} %slice.117), channel_id=1, source_target_pairs={{0,1},{1,2},{2,3},{3,4},{4,5},{5,6},{6,7},{7,8},{8,9},{9,10},{10,1... | collective-permute-start | bytes 6291464 | tf_op jit(solution)/shard_map/ppermute | solution.py:14
  84.1 65.8 %collective-permute-start.2 = (bf16[512,2048]{1,0:T(8,128)(2,1)}, bf16[512,2048]{1,0:T(8,128)(2,1)S(1)}, u32[]{:S(2)}, u32[]{:S(2)}) collective-permute-start(bf16[512,2048]{1,0:T(8,128)(2,1)} %slice.117), channel_id=1, source_target_pairs={{0,15},{1,0},{2,1},{3,2},{4,3},{5,4},{6,5},{7,6},{8,7},{9,8},{10,9... | collective-permute-start | bytes 6291464 | tf_op jit(solution)/shard_map/ppermute | solution.py:14
  84.2 52.7 %collective-permute-start.4 = (s32[3,512]{1,0:T(4,128)S(1)}, s32[3,512]{1,0:T(4,128)S(1)}, u32[]{:S(2)}, u32[]{:S(2)}) collective-permute-start(s32[3,512]{1,0:T(4,128)S(1)} %pad_add_fusion), channel_id=1, source_target_pairs={{0,1},{1,2},{2,3},{3,4},{4,5},{5,6},{6,7},{7,8},{8,9},{9,10},{10,1... | collective-permute-start | bytes 18440 | tf_op jit(solution)/shard_map/ppermute | solution.py:14
  85.9 54.0 %collective-permute-start.6 = (s32[3,512]{1,0:T(4,128)S(1)}, s32[3,512]{1,0:T(4,128)S(1)}, u32[]{:S(2)}, u32[]{:S(2)}) collective-permute-start(s32[3,512]{1,0:T(4,128)S(1)} %pad_add_fusion), channel_id=1, source_target_pairs={{0,15},{1,0},{2,1},{3,2},{4,3},{5,4},{6,5},{7,6},{8,7},{9,8},{10,9... | collective-permute-start | bytes 18440 | tf_op jit(solution)/shard_map/ppermute | solution.py:14
  137.0 4.7 collective-permute-start.5
  139.9 4.3 collective-permute-start.7
  139.9 47.5 %collective-permute-start.1 = (bf16[512,2048]{1,0:T(8,128)(2,1)}, bf16[512,2048]{1,0:T(8,128)(2,1)}, u32[]{:S(2)}, u32[]{:S(2)}) collective-permute-start(bf16[512,2048]{1,0:T(8,128)(2,1)} %collective-permute-done), channel_id=1, source_target_pairs={{0,1},{1,2},{2,3},{3,4},{4,5},{5,6},{6,7},{7,8},{8,9},{9,10},{10,1... | collective-permute-start | bytes 6291464 | tf_op jit(solution)/shard_map/ppermute | solution.py:14
  149.9 48.5 %collective-permute-start.3 = (bf16[512,2048]{1,0:T(8,128)(2,1)S(1)}, bf16[512,2048]{1,0:T(8,128)(2,1)}, u32[]{:S(2)}, u32[]{:S(2)}) collective-permute-start(bf16[512,2048]{1,0:T(8,128)(2,1)S(1)} %collective-permute-done.2), channel_id=1, source_target_pairs={{0,15},{1,0},{2,1},{3,2},{4,3},{5,4},{6,5},{7,6},{8,7},{9,8},{10,9... | collective-permute-start | bytes 6291464 | tf_op jit(solution)/shard_map/ppermute | solution.py:14
  210.9 8.0 %copy-start.5 = (bf16[512,1024]{0,1:T(8,128)(2,1)S(1)}, bf16[512,1024]{0,1:T(8,128)(2,1)}, u32[]{:S(2)}) copy-start(bf16[512,1024]{0,1:T(8,128)(2,1)} %copy.21) | copy-start | bytes 3145732
  218.9 10.1 %copy-start.3 = (bf16[2560,1024]{0,1:T(8,128)(2,1)S(1)}, bf16[2560,1024]{0,1:T(8,128)(2,1)}, u32[]{:S(2)}) copy-start(bf16[2560,1024]{0,1:T(8,128)(2,1)} %copy.22) | copy-start | bytes 15728644
  255.1 7.9 %copy-start.4 = (pred[512,2560]{1,0:T(8,128)(4,1)S(1)}, pred[512,2560]{1,0:T(8,128)(4,1)}, u32[]{:S(2)}) copy-start(pred[512,2560]{1,0:T(8,128)(4,1)} %fusion.41) | copy-start | bytes 3932164
  416.5 29.5 %copy-start.10 = (f32[4]{0:T(128)S(1)}, f32[4]{0:T(128)}, u32[]{:S(2)}) copy-start(f32[4]{0:T(128)} %get-tuple-element.10) | copy-start | bytes 52
  416.5 29.5 %copy-start.11 = (f32[4]{0:T(128)S(1)}, f32[4]{0:T(128)}, u32[]{:S(2)}) copy-start(f32[4]{0:T(128)} %get-tuple-element.15) | copy-start | bytes 52
  477.6 33.9 %copy-start.1 = (bf16[512,1024]{1,0:T(8,128)(2,1)S(1)}, bf16[512,1024]{1,0:T(8,128)(2,1)}, u32[]{:S(2)}) copy-start(bf16[512,1024]{1,0:T(8,128)(2,1)} %param.7) | copy-start | bytes 3145732
Sparse Core Ops, SparseCore 0:
  9.6 64.3 all-gather.2
  88.7 55.8 all-gather.4
where the time goes:
time: 523 us; the launch traced here: 519 us
  matrix products  165 us (32%)
  waiting for transfers between devices  151 us (29%)
  other arithmetic  133 us (25%)
  local copies, waits for them, and re-layouts  45.9 us (9%)
  between operations  13.9 us (3%)
  starting transfers between devices  9.53 us (2%)
    sub x4, other arithmetic, local(): weight = jnp.where(allowed[None, :, :], jnp.exp(score - peak), 0.0)  126 us
    dot_general x4, matrix products, local(): jnp.einsum('hqk,khe->qhe', weight_bf, v_grp, preferred_element_type=jnp.f...  119 us
    ppermute x8, waiting for transfers between devices, passed_along(): lax.ppermute(value, axis, [(i, (i + by) % devices) for i in range(devices)])  83.3 us
    all_gather x1, waiting for transfers between devices, local(): lax.all_gather(w_qkv, 'ctx', axis=0, tiled=True)  66.7 us
    dot_general x4, matrix products, local(): jnp.einsum('qhe,khe->hqk', q_grp, k_grp, preferred_element_type=jnp.float32)  36.2 us
    slice x2, local copies, waits for them, and re-layouts, local(): key_heads = win_kv[:, :width].reshape(span, heads, hsize)  17.3 us
    unnamed x31, local copies, waits for them, and re-layouts  12.8 us
  transfers between devices with their start and end apart: 10, of which 5 were waited for; matrix products, arithmetic and copies ran while one was open for 64% of the time, Pallas kernels for 0%

commit v1 on v0

--- a/solution.py
+++ b/solution.py
@@ -3,6 +3,28 @@
 import jax.numpy as jnp
 from jax import lax
 from jax.sharding import PartitionSpec as P
+
+
+def in_order(parts, dim):
+    parts = jnp.moveaxis(parts, 0, dim)
+    shape = parts.shape
+    return parts.reshape(*shape[:dim], shape[dim] * shape[dim + 1], *shape[dim + 2 :])
+
+
+def ring_gather(array, axis, dim):
+    devices = lax.axis_size(axis)
+    pairs = [(i, (i + 1) % devices) for i in range(devices)]
+    back = [(b, a) for a, b in pairs]
+    lower, upper = ([], [])
+    for step in range(devices - 1):
+        if step % 2 == 0:
+            lower.append(lax.ppermute(lower[-1] if lower else array, axis, pairs))
+        else:
+            upper.append(lax.ppermute(upper[-1] if upper else array, axis, back))
+    blocks = jnp.stack([*lower[::-1], array, *upper])
+    shift = lax.axis_index(axis) - len(lower)
+    blocks = blocks[(jnp.arange(devices) - shift) % devices]
+    return in_order(blocks, dim)
 
 
 def as_sent(value):
@@ -35,11 +57,7 @@
     center = lax.axis_index("ctx")
     count = lax.axis_size("ctx")
     columns = tokens
-    qkv = jnp.dot(
-        columns,
-        lax.all_gather(w_qkv, "ctx", axis=0, tiled=True),
-        preferred_element_type=jnp.float32,
-    )
+    qkv = jnp.dot(columns, ring_gather(w_qkv, "ctx", 0), preferred_element_type=jnp.float32)
     qkv = qkv.astype(jnp.bfloat16)
     query = qkv[:, :width]
     keyval = qkv[:, width:]

time: 523 us -> 548 us (1.048)
  starting transfers between devices: 9.53 us -> 29.9 us
    all_gather x1 -> x0, waiting for transfers between devices: 66.7 us -> none  [local(): lax.all_gather(w_qkv, 'ctx', axis=0, tiled=True)]
    ppermute x0 -> x15, waiting for transfers between devices: none -> 59 us  [the longest x8 57.2 us: ring_gather(): lower.append(lax.ppermute(lower[-1] if lower else array, axis, pairs))]
    ppermute x0 -> x15, starting transfers between devices: none -> 21.2 us  [the longest x8 20 us: ring_gather(): lower.append(lax.ppermute(lower[-1] if lower else array, axis, pairs))]
    unnamed x31 -> x62, local copies, waits for them, and re-layouts: 12.8 us -> 30 us
    slice x2 -> x1, local copies, waits for them, and re-layouts: 17.3 us -> 8.62 us  [local(): key_heads = win_kv[:, :width].reshape(span, heads, hsize)]
    slice x1 -> x0, local copies, waits for them, and re-layouts: 7.89 us -> none  [local(): value_heads = win_kv[:, width:].reshape(span, heads, hsize)]
    gather x0 -> x1, local copies, waits for them, and re-layouts: none -> 6.38 us  [ring_gather(): blocks = blocks[(jnp.arange(devices) - shift) % devices]]
  transfers between devices with their start and end apart: 10 -> 24, of which waited for: 5 -> 17; matrix products, arithmetic and copies ran while one was open for 64% -> 61% of each run, Pallas kernels for 0% -> 0%
where the time goes in v1:
time: 548 us; the launch traced here: 540 us
  matrix products  166 us (30%)
  waiting for transfers between devices  146 us (27%)
  other arithmetic  133 us (24%)
  local copies, waits for them, and re-layouts  50.7 us (9%)
  starting transfers between devices  29.9 us (5%)
  between operations  13.9 us (3%)
    sub x4, other arithmetic, local(): weight = jnp.where(allowed[None, :, :], jnp.exp(score - peak), 0.0)  126 us
    dot_general x4, matrix products, local(): jnp.einsum('hqk,khe->qhe', weight_bf, v_grp, preferred_element_type=jnp.f...  119 us
    ppermute x8, waiting for transfers between devices, passed_along(): lax.ppermute(value, axis, [(i, (i + by) % devices) for i in range(devices)])  86.6 us
    ppermute x8, waiting for transfers between devices, ring_gather(): lower.append(lax.ppermute(lower[-1] if lower else array, axis, pairs))  57.2 us
    dot_general x4, matrix products, local(): jnp.einsum('qhe,khe->hqk', q_grp, k_grp, preferred_element_type=jnp.float32)  36.8 us
    unnamed x62, local copies, waits for them, and re-layouts  30 us
    ppermute x8, starting transfers between devices, ring_gather(): lower.append(lax.ppermute(lower[-1] if lower else array, axis, pairs))  20 us
  transfers between devices with their start and end apart: 24, of which 17 were waited for; matrix products, arithmetic and copies ran while one was open for 61% of the time, Pallas kernels for 0%

profile of v1, /device:TPU:1, one launch (start us, length us, event | category | flops | bytes accessed | tf_op | source)
XLA Modules:
  0.0 539.7 jit_solution(9626187341493043082)
XLA Ops:
  6.5 2.6 collective-permute-start
  9.2 5.0 collective-permute-done
  14.2 2.4 collective-permute-start.1
  16.6 1.2 collective-permute-start.8
  17.7 7.8 %collective-permute-done.1 = bf16[64,3072]{1,0:T(8,128)(2,1)S(1)} collective-permute-done((bf16[64,3072]{1,0:T(8,128)(2,1)S(1)}, bf16[64,3072]{1,0:T(8,128)(2,1)S(1)}, u32[]{:S(2)}, u32[]{:S(2)}) %collective-permute-start.1) | collective-permute-done | bytes 393248 | tf_op jit(solution)/shard_map/ppermute | solution.py:21
  25.5 2.5 collective-permute-start.2
  28.2 8.7 %collective-permute-done.2 = bf16[64,3072]{1,0:T(8,128)(2,1)S(1)} collective-permute-done((bf16[64,3072]{1,0:T(8,128)(2,1)S(1)}, bf16[64,3072]{1,0:T(8,128)(2,1)S(1)}, u32[]{:S(2)}, u32[]{:S(2)}) %collective-permute-start.2) | collective-permute-done | bytes 393248 | tf_op jit(solution)/shard_map/ppermute | solution.py:21
  36.9 2.5 collective-permute-start.3
  39.6 8.0 %collective-permute-done.3 = bf16[64,3072]{1,0:T(8,128)(2,1)S(1)} collective-permute-done((bf16[64,3072]{1,0:T(8,128)(2,1)S(1)}, bf16[64,3072]{1,0:T(8,128)(2,1)S(1)}, u32[]{:S(2)}, u32[]{:S(2)}) %collective-permute-start.3) | collective-permute-done | bytes 393248 | tf_op jit(solution)/shard_map/ppermute | solution.py:21
  47.6 2.5 collective-permute-start.4
  50.1 1.0 collective-permute-done.10
  51.8 7.2 %collective-permute-done.4 = bf16[64,3072]{1,0:T(8,128)(2,1)S(1)} collective-permute-done((bf16[64,3072]{1,0:T(8,128)(2,1)S(1)}, bf16[64,3072]{1,0:T(8,128)(2,1)S(1)}, u32[]{:S(2)}, u32[]{:S(2)}) %collective-permute-start.4) | collective-permute-done | bytes 393248 | tf_op jit(solution)/shard_map/ppermute | solution.py:21
  59.0 2.5 collective-permute-start.5
  62.2 6.3 %collective-permute-done.5 = bf16[64,3072]{1,0:T(8,128)(2,1)S(1)} collective-permute-done((bf16[64,3072]{1,0:T(8,128)(2,1)S(1)}, bf16[64,3072]{1,0:T(8,128)(2,1)S(1)}, u32[]{:S(2)}, u32[]{:S(2)}) %collective-permute-start.5) | collective-permute-done | bytes 393248 | tf_op jit(solution)/shard_map/ppermute | solution.py:21
  68.5 2.5 collective-permute-start.6
  71.3 7.3 %collective-permute-done.6 = bf16[64,3072]{1,0:T(8,128)(2,1)} collective-permute-done((bf16[64,3072]{1,0:T(8,128)(2,1)S(1)}, bf16[64,3072]{1,0:T(8,128)(2,1)}, u32[]{:S(2)}, u32[]{:S(2)}) %collective-permute-start.6) | collective-permute-done | bytes 393248 | tf_op jit(solution)/shard_map/ppermute | solution.py:21
  78.6 2.6 collective-permute-start.7
  81.3 6.9 %collective-permute-done.7 = bf16[64,3072]{1,0:T(8,128)(2,1)} collective-permute-done((bf16[64,3072]{1,0:T(8,128)(2,1)}, bf16[64,3072]{1,0:T(8,128)(2,1)}, u32[]{:S(2)}, u32[]{:S(2)}) %collective-permute-start.7) | collective-permute-done | bytes 393248 | tf_op jit(solution)/shard_map/ppermute | solution.py:21
  88.2 1.8 bitcast_dynamic-update-slice_fusion.15
  90.0 1.8 bitcast_dynamic-update-slice_fusion.14
  91.8 1.8 bitcast_dynamic-update-slice_fusion.13
  93.5 1.8 bitcast_dynamic-update-slice_fusion.12
  95.3 1.8 bitcast_dynamic-update-slice_fusion.11
  97.1 0.8 bitcast_dynamic-update-slice_fusion.10
  97.9 0.8 bitcast_dynamic-update-slice_fusion.9
  98.7 0.8 bitcast_dynamic-update-slice_fusion.8
  101.8 0.8 bitcast_dynamic-update-slice_fusion.4
  102.6 0.8 bitcast_dynamic-update-slice_fusion.3
  103.4 1.8 bitcast_dynamic-update-slice_fusion.2
  105.2 1.8 bitcast_dynamic-update-slice_fusion.1
  107.7 6.4 %gather_fusion = bf16[16,64,3072]{2,1,0:T(8,128)(2,1)} fusion(bf16[16,64,3072]{2,1,0:T(8,128)(2,1)} %bitcast_dynamic-update-slice_fusion, s32[1024]{0:T(1024)S(1)} %pad_clamp_fusion), kind=kCustom, calls=%fused_computation | custom fusion | bytes 12582976 | tf_op jit(solution)/shard_map/gather | solution.py:26
  114.1 6.6 %fusion.42 = bf16[512,3072]{0,1:T(8,128)(2,1)S(1)} fusion(bf16[1024,3072]{1,0:T(8,128)(2,1)} %bitcast.100, bf16[512,1024]{1,0:T(8,128)(2,1)S(1)} %copy-done), kind=kOutput, calls=%fused_computation.53 | convolution fusion | flops 3222798336 | bytes 10485760 | tf_op jit(solution)/shard_map/dot_general | solution.py:60
  120.8 1.7 copy-done.2
  122.5 1.5 slice.119
  124.0 2.5 collective-permute-start.15
  126.5 1.8 collective-permute-start.19
  129.3 48.0 %collective-permute-done.19 = s32[3,512]{1,0:T(4,128)S(1)} collective-permute-done((s32[3,512]{1,0:T(4,128)S(1)}, s32[3,512]{1,0:T(4,128)S(1)}, u32[]{:S(2)}, u32[]{:S(2)}) %collective-permute-start.19) | collective-permute-done | bytes 6176 | tf_op jit(solution)/shard_map/ppermute | solution.py:36
  177.3 2.5 collective-permute-start.20
  179.8 1.7 collective-permute-done.21
  181.4 1.7 collective-permute-start.16
  183.2 2.4 collective-permute-done.22
  185.7 5.5 %fusion.41 = pred[512,2560]{1,0:T(8,128)(4,1)} fusion(s32[2560]{0:T(1024)S(1)} %iota_add_fusion, s32[512]{0:T(512)S(1)} %iota_add_fusion.1, s32[2560]{0:T(1024)S(1)} %get-tuple-element.7, s32[2560]{0:T(1024)S(1)} %get-tuple-element.5, s32[512]{0:T(512)S(1)} %copy-done.14, s32[512]{0:T(512)S(1)} %copy-done.15, pred[2560]{0:T(1024)(128)(4,1)S(1)} %compare_and_fusion), kind=kLoop, calls=%fused_computation.51 | loop fusion | flops 10485760 | bytes 1350144 | tf_op jit(solution)/shard_map/and | solution.py:74
  191.2 1.9 broadcast_compare_fusion
  193.1 1.3 slice.123
  194.4 34.5 %collective-permute-done.16 = bf16[512,2048]{0,1:T(8,128)(2,1)S(1)} collective-permute-done((bf16[512,2048]{0,1:T(8,128)(2,1)}, bf16[512,2048]{0,1:T(8,128)(2,1)S(1)}, u32[]{:S(2)}, u32[]{:S(2)}) %collective-permute-start.16) | collective-permute-done | bytes 2097184 | tf_op jit(solution)/shard_map/ppermute | solution.py:36
  228.9 1.6 constant_dynamic-update-slice_fusion.4
  230.5 3.1 constant_dynamic-update-slice_fusion.3
  233.7 1.6 constant_dynamic-update-slice_fusion.2
  235.2 1.6 constant_dynamic-update-slice_fusion.1
  236.9 1.5 constant_dynamic-update-slice_fusion
  238.4 8.6 %fusion.121 = (bf16[2560,1024]{0,1:T(8,128)(2,1)}, bf16[2560,1024]{0,1:T(8,128)(2,1)}) fusion(bf16[2560,2048]{0,1:T(8,128)(2,1)} %constant_dynamic-update-slice_fusion), kind=kLoop, calls=%fused_computation.149 | loop fusion | bytes 20971520 | tf_op jit(solution)/shard_map/slice | solution.py:77
  247.0 10.6 %fusion.49 = f32[4,512,2560]{2,1,0:T(8,128)} fusion(bf16[512,16,64]{0,2,1:T(8,128)(2,1)S(1)} %bitcast.110, bf16[2560,16,64]{0,2,1:T(8,128)(2,1)} %bitcast.105), kind=kOutput, calls=%fused_computation.62 | convolution fusion | flops 671088640 | bytes 23330816 | tf_op jit(solution)/shard_map/qhe,khe->hqk/dot_general | solution.py:92
  257.6 8.6 %fusion.47 = f32[4,512,2560]{2,1,0:T(8,128)} fusion(bf16[512,16,64]{0,2,1:T(8,128)(2,1)S(1)} %bitcast.111, bf16[2560,16,64]{0,2,1:T(8,128)(2,1)S(1)} %bitcast.106), kind=kOutput, calls=%fused_computation.60 | convolution fusion | flops 671088640 | bytes 23330816 | tf_op jit(solution)/shard_map/qhe,khe->hqk/dot_general | solution.py:92
  266.3 8.8 %fusion.45 = f32[4,512,2560]{2,1,0:T(8,128)} fusion(bf16[512,16,64]{0,2,1:T(8,128)(2,1)S(1)} %bitcast.112, bf16[2560,16,64]{0,2,1:T(8,128)(2,1)S(1)} %bitcast.107), kind=kOutput, calls=%fused_computation.58 | convolution fusion | flops 671088640 | bytes 23330816 | tf_op jit(solution)/shard_map/qhe,khe->hqk/dot_general | solution.py:92
  275.1 8.7 %fusion.43 = f32[4,512,2560]{2,1,0:T(8,128)} fusion(bf16[512,16,64]{0,2,1:T(8,128)(2,1)S(1)} %bitcast.113, bf16[2560,16,64]{0,2,1:T(8,128)(2,1)S(1)} %bitcast.108), kind=kOutput, calls=%fused_computation.56 | convolution fusion | flops 671088640 | bytes 23330816 | tf_op jit(solution)/shard_map/qhe,khe->hqk/dot_general | solution.py:92
  283.8 31.2 %fusion.125 = f32[4,512]{1,0:T(4,128)S(1)} fusion(f32[4,512,2560]{2,1,0:T(8,128)} %fusion.49, f32[4]{0:T(128)S(1)} %get-tuple-element.15, f32[4]{0:T(128)S(1)} %get-tuple-element.10, pred[512,2560]{1,0:T(8,128)(4,1)} %broadcast_compare_fusion, pred[512,2560]{1,0:T(8,128)(4,1)S(1)} %copy-done.5), kind=kOutput, calls=%fused_computation.153 | output fusion | flops 36702720 | bytes 23601184 | tf_op jit(solution)/shard_map/sub | solution.py:97
  315.0 29.8 %fusion.84 = bf16[512,4,64]{0,2,1:T(8,128)(2,1)S(1)} fusion(bf16[2560,16,64]{0,2,1:T(8,128)(2,1)} %bitcast.101, f32[4,512,2560]{2,1,0:T(8,128)} %fusion.49, f32[4]{0:T(128)S(1)} %get-tuple-element.15, f32[4]{0:T(128)S(1)} %get-tuple-element.10, pred[512,2560]{1,0:T(8,128)(4,1)} %broadcast_compare_fusion, pred[512,2560]{1,0:T(8,128)(4,1)S(1)} %copy-done.5, ...), kind=kOutput, calls=%fused_computation.76 | convolution fusion | flops 708055552 | bytes 29106208 | tf_op jit(solution)/shard_map/hqk,khe->qhe/dot_general | solution.py:100
  344.8 31.6 %fusion.124 = f32[4,512]{1,0:T(4,128)S(1)} fusion(f32[4,512,2560]{2,1,0:T(8,128)} %fusion.47, f32[4]{0:T(128)S(1)} %get-tuple-element.13, f32[4]{0:T(128)S(1)} %get-tuple-element.14, pred[512,2560]{1,0:T(8,128)(4,1)} %broadcast_compare_fusion, pred[512,2560]{1,0:T(8,128)(4,1)S(1)} %copy-done.5), kind=kOutput, calls=%fused_computation.152 | output fusion | flops 36702720 | bytes 23601184 | tf_op jit(solution)/shard_map/sub | solution.py:97
  376.4 29.5 %fusion.78 = bf16[512,4,64]{0,2,1:T(8,128)(2,1)S(1)} fusion(bf16[2560,16,64]{0,2,1:T(8,128)(2,1)} %bitcast.102, f32[4,512,2560]{2,1,0:T(8,128)} %fusion.47, f32[4]{0:T(128)S(1)} %get-tuple-element.13, f32[4]{0:T(128)S(1)} %get-tuple-element.14, pred[512,2560]{1,0:T(8,128)(4,1)} %broadcast_compare_fusion, pred[512,2560]{1,0:T(8,128)(4,1)S(1)} %copy-done.5, ...), kind=kOutput, calls=%fused_computation.74 | convolution fusion | flops 708055552 | bytes 29106208 | tf_op jit(solution)/shard_map/hqk,khe->qhe/dot_general | solution.py:100
  405.9 31.3 %fusion.123 = f32[4,512]{1,0:T(4,128)S(1)} fusion(f32[4,512,2560]{2,1,0:T(8,128)} %fusion.45, f32[4]{0:T(128)S(1)} %get-tuple-element.11, f32[4]{0:T(128)S(1)} %get-tuple-element.12, pred[512,2560]{1,0:T(8,128)(4,1)} %broadcast_compare_fusion, pred[512,2560]{1,0:T(8,128)(4,1)S(1)} %copy-done.5), kind=kOutput, calls=%fused_computation.151 | output fusion | flops 36702720 | bytes 23601184 | tf_op jit(solution)/shard_map/sub | solution.py:97
  437.3 29.9 %fusion.72 = bf16[512,4,64]{0,2,1:T(8,128)(2,1)S(1)} fusion(bf16[2560,16,64]{0,2,1:T(8,128)(2,1)} %bitcast.103, f32[4,512,2560]{2,1,0:T(8,128)} %fusion.45, f32[4]{0:T(128)S(1)} %get-tuple-element.11, f32[4]{0:T(128)S(1)} %get-tuple-element.12, pred[512,2560]{1,0:T(8,128)(4,1)} %broadcast_compare_fusion, pred[512,2560]{1,0:T(8,128)(4,1)S(1)} %copy-done.5, ...), kind=kOutput, calls=%fused_computation.72 | convolution fusion | flops 708055552 | bytes 29106208 | tf_op jit(solution)/shard_map/hqk,khe->qhe/dot_general | solution.py:100
  467.2 31.5 %fusion.122 = f32[4,512]{1,0:T(4,128)S(1)} fusion(f32[4,512,2560]{2,1,0:T(8,128)} %fusion.43, f32[4]{0:T(128)S(1)} %copy-done.18, f32[4]{0:T(128)S(1)} %copy-done.19, pred[512,2560]{1,0:T(8,128)(4,1)} %broadcast_compare_fusion, pred[512,2560]{1,0:T(8,128)(4,1)S(1)} %copy-done.5), kind=kOutput, calls=%fused_computation.150 | output fusion | flops 36702720 | bytes 23601184 | tf_op jit(solution)/shard_map/sub | solution.py:97
  498.7 29.9 %fusion.66 = bf16[512,4,64]{0,2,1:T(8,128)(2,1)S(1)} fusion(bf16[2560,16,64]{0,2,1:T(8,128)(2,1)} %bitcast.104, f32[4,512,2560]{2,1,0:T(8,128)} %fusion.43, f32[4]{0:T(128)S(1)} %copy-done.18, f32[4]{0:T(128)S(1)} %copy-done.19, pred[512,2560]{1,0:T(8,128)(4,1)} %broadcast_compare_fusion, pred[512,2560]{1,0:T(8,128)(4,1)S(1)} %copy-done.5, ...), kind=kOutput, calls=%fused_computation.70 | convolution fusion | flops 708055552 | bytes 29106208 | tf_op jit(solution)/shard_map/hqk,khe->qhe/dot_general | solution.py:100
  528.8 3.8 convolution_convert_fusion.1
  (80 shorter events, 6.7 us)
Async XLA Ops:
  6.5 107.6 %copy-start = (bf16[512,1024]{1,0:T(8,128)(2,1)S(1)}, bf16[512,1024]{1,0:T(8,128)(2,1)}, u32[]{:S(2)}) copy-start(bf16[512,1024]{1,0:T(8,128)(2,1)} %param.7) | copy-start | bytes 3145732
  6.5 92.9 %copy-start.6 = (bf16[64,3072]{1,0:T(8,128)(2,1)S(1)}, bf16[64,3072]{1,0:T(8,128)(2,1)}, u32[]{:S(2)}) copy-start(bf16[64,3072]{1,0:T(8,128)(2,1)} %param.8) | copy-start | bytes 1179652
  6.5 522.2 %all-gather.2.cloned.1.call-start = ((), (), s32[]{:S(2)}) async-start(), calls=%async_computation | async-start | bytes 2228224 | tf_op jit(solution)/shard_map/all_gather | solution.py:106
  6.5 7.7 %collective-permute-start = (bf16[64,3072]{1,0:T(8,128)(2,1)}, bf16[64,3072]{1,0:T(8,128)(2,1)S(1)}, u32[]{:S(2)}, u32[]{:S(2)}) collective-permute-start(bf16[64,3072]{1,0:T(8,128)(2,1)} %param.8), channel_id=1, source_target_pairs={{0,1},{1,2},{2,3},{3,4},{4,5},{5,6},{6,7},{7,8},{8,9},{9,10},{10,1... | collective-permute-start | bytes 1179656 | tf_op jit(solution)/shard_map/ppermute | solution.py:21
  14.2 11.3 %collective-permute-start.1 = (bf16[64,3072]{1,0:T(8,128)(2,1)S(1)}, bf16[64,3072]{1,0:T(8,128)(2,1)S(1)}, u32[]{:S(2)}, u32[]{:S(2)}) collective-permute-start(bf16[64,3072]{1,0:T(8,128)(2,1)S(1)} %collective-permute-done), channel_id=1, source_target_pairs={{0,1},{1,2},{2,3},{3,4},{4,5},{5,6},{6,7},{7,8},{8,9},{9,10},{10,1... | collective-permute-start | bytes 1179656 | tf_op jit(solution)/shard_map/ppermute | solution.py:21
  16.6 11.6 %collective-permute-start.8 = (bf16[64,3072]{1,0:T(8,128)(2,1)}, bf16[64,3072]{1,0:T(8,128)(2,1)S(1)}, u32[]{:S(2)}, u32[]{:S(2)}) collective-permute-start(bf16[64,3072]{1,0:T(8,128)(2,1)} %param.8), channel_id=1, source_target_pairs={{1,0},{2,1},{3,2},{4,3},{5,4},{6,5},{7,6},{8,7},{9,8},{10,9},{11,1... | collective-permute-start | bytes 1179656 | tf_op jit(solution)/shard_map/ppermute | solution.py:23
  25.5 11.4 %collective-permute-start.2 = (bf16[64,3072]{1,0:T(8,128)(2,1)S(1)}, bf16[64,3072]{1,0:T(8,128)(2,1)S(1)}, u32[]{:S(2)}, u32[]{:S(2)}) collective-permute-start(bf16[64,3072]{1,0:T(8,128)(2,1)S(1)} %collective-permute-done.1), channel_id=1, source_target_pairs={{0,1},{1,2},{2,3},{3,4},{4,5},{5,6},{6,7},{7,8},{8,9},{9,10},{10,1... | collective-permute-start | bytes 1179656 | tf_op jit(solution)/shard_map/ppermute | solution.py:21
  28.2 11.4 %collective-permute-start.9 = (bf16[64,3072]{1,0:T(8,128)(2,1)S(1)}, bf16[64,3072]{1,0:T(8,128)(2,1)S(1)}, u32[]{:S(2)}, u32[]{:S(2)}) collective-permute-start(bf16[64,3072]{1,0:T(8,128)(2,1)S(1)} %collective-permute-done.8), channel_id=1, source_target_pairs={{1,0},{2,1},{3,2},{4,3},{5,4},{6,5},{7,6},{8,7},{9,8},{10,9},{11,1... | collective-permute-start | bytes 1179656 | tf_op jit(solution)/shard_map/ppermute | solution.py:23
  36.9 10.6 %collective-permute-start.3 = (bf16[64,3072]{1,0:T(8,128)(2,1)S(1)}, bf16[64,3072]{1,0:T(8,128)(2,1)S(1)}, u32[]{:S(2)}, u32[]{:S(2)}) collective-permute-start(bf16[64,3072]{1,0:T(8,128)(2,1)S(1)} %collective-permute-done.2), channel_id=1, source_target_pairs={{0,1},{1,2},{2,3},{3,4},{4,5},{5,6},{6,7},{7,8},{8,9},{9,10},{10,1... | collective-permute-start | bytes 1179656 | tf_op jit(solution)/shard_map/ppermute | solution.py:21
  39.6 11.4 %collective-permute-start.10 = (bf16[64,3072]{1,0:T(8,128)(2,1)S(1)}, bf16[64,3072]{1,0:T(8,128)(2,1)S(1)}, u32[]{:S(2)}, u32[]{:S(2)}) collective-permute-start(bf16[64,3072]{1,0:T(8,128)(2,1)S(1)} %collective-permute-done.9), channel_id=1, source_target_pairs={{1,0},{2,1},{3,2},{4,3},{5,4},{6,5},{7,6},{8,7},{9,8},{10,9},{11,1... | collective-permute-start | bytes 1179656 | tf_op jit(solution)/shard_map/ppermute | solution.py:23
  47.6 23.7 %copy-start.11 = (bf16[64,3072]{1,0:T(8,128)(2,1)}, bf16[64,3072]{1,0:T(8,128)(2,1)S(1)}, u32[]{:S(2)}) copy-start(bf16[64,3072]{1,0:T(8,128)(2,1)S(1)} %collective-permute-done.3) | copy-start | bytes 1179652
  47.6 11.4 %collective-permute-start.4 = (bf16[64,3072]{1,0:T(8,128)(2,1)S(1)}, bf16[64,3072]{1,0:T(8,128)(2,1)S(1)}, u32[]{:S(2)}, u32[]{:S(2)}) collective-permute-start(bf16[64,3072]{1,0:T(8,128)(2,1)S(1)} %collective-permute-done.3), channel_id=1, source_target_pairs={{0,1},{1,2},{2,3},{3,4},{4,5},{5,6},{6,7},{7,8},{8,9},{9,10},{10,1... | collective-permute-start | bytes 1179656 | tf_op jit(solution)/shard_map/ppermute | solution.py:21
  51.0 0.7 copy-start.7
  51.8 9.7 %collective-permute-start.11 = (bf16[64,3072]{1,0:T(8,128)(2,1)S(1)}, bf16[64,3072]{1,0:T(8,128)(2,1)S(1)}, u32[]{:S(2)}, u32[]{:S(2)}) collective-permute-start(bf16[64,3072]{1,0:T(8,128)(2,1)S(1)} %collective-permute-done.10), channel_id=1, source_target_pairs={{1,0},{2,1},{3,2},{4,3},{5,4},{6,5},{7,6},{8,7},{9,8},{10,9},{11,1... | collective-permute-start | bytes 1179656 | tf_op jit(solution)/shard_map/ppermute | solution.py:23
  59.0 12.3 %copy-start.12 = (bf16[64,3072]{1,0:T(8,128)(2,1)}, bf16[64,3072]{1,0:T(8,128)(2,1)S(1)}, u32[]{:S(2)}) copy-start(bf16[64,3072]{1,0:T(8,128)(2,1)S(1)} %collective-permute-done.4) | copy-start | bytes 1179652
  59.0 9.6 %collective-permute-start.5 = (bf16[64,3072]{1,0:T(8,128)(2,1)S(1)}, bf16[64,3072]{1,0:T(8,128)(2,1)S(1)}, u32[]{:S(2)}, u32[]{:S(2)}) collective-permute-start(bf16[64,3072]{1,0:T(8,128)(2,1)S(1)} %collective-permute-done.4), channel_id=1, source_target_pairs={{0,1},{1,2},{2,3},{3,4},{4,5},{5,6},{6,7},{7,8},{8,9},{9,10},{10,1... | collective-permute-start | bytes 1179656 | tf_op jit(solution)/shard_map/ppermute | solution.py:21
  61.5 0.7 copy-start.9
  62.2 9.1 %collective-permute-start.12 = (bf16[64,3072]{1,0:T(8,128)(2,1)S(1)}, bf16[64,3072]{1,0:T(8,128)(2,1)}, u32[]{:S(2)}, u32[]{:S(2)}) collective-permute-start(bf16[64,3072]{1,0:T(8,128)(2,1)S(1)} %collective-permute-done.11), channel_id=1, source_target_pairs={{1,0},{2,1},{3,2},{4,3},{5,4},{6,5},{7,6},{8,7},{9,8},{10,9},{11,1... | collective-permute-start | bytes 1179656 | tf_op jit(solution)/shard_map/ppermute | solution.py:23
  68.5 10.1 %copy-start.13 = (bf16[64,3072]{1,0:T(8,128)(2,1)}, bf16[64,3072]{1,0:T(8,128)(2,1)S(1)}, u32[]{:S(2)}) copy-start(bf16[64,3072]{1,0:T(8,128)(2,1)S(1)} %collective-permute-done.5) | copy-start | bytes 1179652
  68.5 10.0 %collective-permute-start.6 = (bf16[64,3072]{1,0:T(8,128)(2,1)S(1)}, bf16[64,3072]{1,0:T(8,128)(2,1)}, u32[]{:S(2)}, u32[]{:S(2)}) collective-permute-start(bf16[64,3072]{1,0:T(8,128)(2,1)S(1)} %collective-permute-done.5), channel_id=1, source_target_pairs={{0,1},{1,2},{2,3},{3,4},{4,5},{5,6},{6,7},{7,8},{8,9},{9,10},{10,1... | collective-permute-start | bytes 1179656 | tf_op jit(solution)/shard_map/ppermute | solution.py:21
  71.3 10.0 %collective-permute-start.13 = (bf16[64,3072]{1,0:T(8,128)(2,1)}, bf16[64,3072]{1,0:T(8,128)(2,1)}, u32[]{:S(2)}, u32[]{:S(2)}) collective-permute-start(bf16[64,3072]{1,0:T(8,128)(2,1)} %collective-permute-done.12), channel_id=1, source_target_pairs={{1,0},{2,1},{3,2},{4,3},{5,4},{6,5},{7,6},{8,7},{9,8},{10,9},{11,1... | collective-permute-start | bytes 1179656 | tf_op jit(solution)/shard_map/ppermute | solution.py:23
  78.6 9.6 %collective-permute-start.7 = (bf16[64,3072]{1,0:T(8,128)(2,1)}, bf16[64,3072]{1,0:T(8,128)(2,1)}, u32[]{:S(2)}, u32[]{:S(2)}) collective-permute-start(bf16[64,3072]{1,0:T(8,128)(2,1)} %collective-permute-done.6), channel_id=1, source_target_pairs={{0,1},{1,2},{2,3},{3,4},{4,5},{5,6},{6,7},{7,8},{8,9},{9,10},{10,1... | collective-permute-start | bytes 1179656 | tf_op jit(solution)/shard_map/ppermute | solution.py:21
  81.2 20.6 %copy-start.8 = (bf16[64,3072]{1,0:T(8,128)(2,1)S(1)}, bf16[64,3072]{1,0:T(8,128)(2,1)}, u32[]{:S(2)}) copy-start(bf16[64,3072]{1,0:T(8,128)(2,1)} %copy-done.7) | copy-start | bytes 1179652
  81.2 21.4 %copy-start.10 = (bf16[64,3072]{1,0:T(8,128)(2,1)S(1)}, bf16[64,3072]{1,0:T(8,128)(2,1)}, u32[]{:S(2)}) copy-start(bf16[64,3072]{1,0:T(8,128)(2,1)} %copy-done.9) | copy-start | bytes 1179652
  81.3 25.7 %collective-permute-start.14 = (bf16[64,3072]{1,0:T(8,128)(2,1)}, bf16[64,3072]{1,0:T(8,128)(2,1)S(1)}, u32[]{:S(2)}, u32[]{:S(2)}) collective-permute-start(bf16[64,3072]{1,0:T(8,128)(2,1)} %collective-permute-done.13), channel_id=1, source_target_pairs={{1,0},{2,1},{3,2},{4,3},{5,4},{6,5},{7,6},{8,7},{9,8},{10,9},{11,1... | collective-permute-start | bytes 1179656 | tf_op jit(solution)/shard_map/ppermute | solution.py:23
  114.1 12.4 %copy-start.14 = (s32[512]{0:T(512)S(1)}, s32[512]{0:T(512)}, u32[]{:S(2)}) copy-start(s32[512]{0:T(512)} %param.13) | copy-start | bytes 6148
  114.1 12.4 %copy-start.15 = (s32[512]{0:T(512)S(1)}, s32[512]{0:T(512)}, u32[]{:S(2)}) copy-start(s32[512]{0:T(512)} %param.11) | copy-start | bytes 6148
  114.1 12.4 %copy-start.16 = (s32[512]{0:T(512)S(1)}, s32[512]{0:T(512)}, u32[]{:S(2)}) copy-start(s32[512]{0:T(512)} %param.12) | copy-start | bytes 6148
  114.1 14.5 %copy-start.17 = (f32[2,16]{1,0:T(2,128)S(1)}, f32[2,16]{1,0:T(2,128)}, u32[]{:S(2)}) copy-start(f32[2,16]{1,0:T(2,128)} %param.10) | copy-start | bytes 388
  120.8 1.7 copy-start.2
  124.0 57.4 %collective-permute-start.15 = (bf16[512,2048]{0,1:T(8,128)(2,1)}, bf16[512,2048]{0,1:T(8,128)(2,1)}, u32[]{:S(2)}, u32[]{:S(2)}) collective-permute-start(bf16[512,2048]{0,1:T(8,128)(2,1)} %slice.119), channel_id=1, source_target_pairs={{0,1},{1,2},{2,3},{3,4},{4,5},{5,6},{6,7},{7,8},{8,9},{9,10},{10,1... | collective-permute-start | bytes 6291464 | tf_op jit(solution)/shard_map/ppermute | solution.py:36
  126.5 64.7 %collective-permute-start.17 = (bf16[512,2048]{0,1:T(8,128)(2,1)}, bf16[512,2048]{0,1:T(8,128)(2,1)S(1)}, u32[]{:S(2)}, u32[]{:S(2)}) collective-permute-start(bf16[512,2048]{0,1:T(8,128)(2,1)} %slice.119), channel_id=1, source_target_pairs={{0,15},{1,0},{2,1},{3,2},{4,3},{5,4},{6,5},{7,6},{8,7},{9,8},{10,9... | collective-permute-start | bytes 6291464 | tf_op jit(solution)/shard_map/ppermute | solution.py:36
  126.5 50.8 %collective-permute-start.19 = (s32[3,512]{1,0:T(4,128)S(1)}, s32[3,512]{1,0:T(4,128)S(1)}, u32[]{:S(2)}, u32[]{:S(2)}) collective-permute-start(s32[3,512]{1,0:T(4,128)S(1)} %pad_add_fusion), channel_id=1, source_target_pairs={{0,1},{1,2},{2,3},{3,4},{4,5},{5,6},{6,7},{7,8},{8,9},{9,10},{10,1... | collective-permute-start | bytes 18440 | tf_op jit(solution)/shard_map/ppermute | solution.py:36
  128.3 53.1 %collective-permute-start.21 = (s32[3,512]{1,0:T(4,128)S(1)}, s32[3,512]{1,0:T(4,128)S(1)}, u32[]{:S(2)}, u32[]{:S(2)}) collective-permute-start(s32[3,512]{1,0:T(4,128)S(1)} %pad_add_fusion), channel_id=1, source_target_pairs={{0,15},{1,0},{2,1},{3,2},{4,3},{5,4},{6,5},{7,6},{8,7},{9,8},{10,9... | collective-permute-start | bytes 18440 | tf_op jit(solution)/shard_map/ppermute | solution.py:36
  177.3 5.9 %collective-permute-start.20 = (s32[3,512]{1,0:T(4,128)S(1)}, s32[3,512]{1,0:T(4,128)S(1)}, u32[]{:S(2)}, u32[]{:S(2)}) collective-permute-start(s32[3,512]{1,0:T(4,128)S(1)} %collective-permute-done.19), channel_id=1, source_target_pairs={{0,1},{1,2},{2,3},{3,4},{4,5},{5,6},{6,7},{7,8},{8,9},{9,10},{10,1... | collective-permute-start | bytes 18440 | tf_op jit(solution)/shard_map/ppermute | solution.py:36
  181.4 4.2 collective-permute-start.22
  181.4 47.5 %collective-permute-start.16 = (bf16[512,2048]{0,1:T(8,128)(2,1)}, bf16[512,2048]{0,1:T(8,128)(2,1)S(1)}, u32[]{:S(2)}, u32[]{:S(2)}) collective-permute-start(bf16[512,2048]{0,1:T(8,128)(2,1)} %collective-permute-done.15), channel_id=1, source_target_pairs={{0,1},{1,2},{2,3},{3,4},{4,5},{5,6},{6,7},{7,8},{8,9},{9,10},{10,1... | collective-permute-start | bytes 6291464 | tf_op jit(solution)/shard_map/ppermute | solution.py:36
  185.7 48.0 %copy-start.3 = (bf16[512,3072]{0,1:T(8,128)(2,1)S(1)}, bf16[512,3072]{0,1:T(8,128)(2,1)}, u32[]{:S(2)}) copy-start(bf16[512,3072]{0,1:T(8,128)(2,1)} %copy-done.2) | copy-start | bytes 9437188
  191.2 45.6 %collective-permute-start.18 = (bf16[512,2048]{0,1:T(8,128)(2,1)S(1)}, bf16[512,2048]{0,1:T(8,128)(2,1)S(1)}, u32[]{:S(2)}, u32[]{:S(2)}) collective-permute-start(bf16[512,2048]{0,1:T(8,128)(2,1)S(1)} %collective-permute-done.17), channel_id=1, source_target_pairs={{0,15},{1,0},{2,1},{3,2},{4,3},{5,4},{6,5},{7,6},{8,7},{9,8},{10,9... | collective-permute-start | bytes 6291464 | tf_op jit(solution)/shard_map/ppermute | solution.py:36
  247.0 10.6 %copy-start.4 = (bf16[2560,1024]{0,1:T(8,128)(2,1)S(1)}, bf16[2560,1024]{0,1:T(8,128)(2,1)}, u32[]{:S(2)}) copy-start(bf16[2560,1024]{0,1:T(8,128)(2,1)} %get-tuple-element.8) | copy-start | bytes 15728644
  275.1 8.7 %copy-start.5 = (pred[512,2560]{1,0:T(8,128)(4,1)S(1)}, pred[512,2560]{1,0:T(8,128)(4,1)}, u32[]{:S(2)}) copy-start(pred[512,2560]{1,0:T(8,128)(4,1)} %fusion.41) | copy-start | bytes 3932164
  437.2 30.0 %copy-start.18 = (f32[4]{0:T(128)S(1)}, f32[4]{0:T(128)}, u32[]{:S(2)}) copy-start(f32[4]{0:T(128)} %get-tuple-element.16) | copy-start | bytes 52
  437.2 30.0 %copy-start.19 = (f32[4]{0:T(128)S(1)}, f32[4]{0:T(128)}, u32[]{:S(2)}) copy-start(f32[4]{0:T(128)} %get-tuple-element.17) | copy-start | bytes 52
  498.7 33.9 %copy-start.1 = (bf16[512,1024]{1,0:T(8,128)(2,1)S(1)}, bf16[512,1024]{1,0:T(8,128)(2,1)}, u32[]{:S(2)}) copy-start(bf16[512,1024]{1,0:T(8,128)(2,1)} %param.7) | copy-start | bytes 3145732
Sparse Core Ops, SparseCore 0:
  128.7 52.1 all-gather.1
